TPU v7x, 512 devices: a whole 4x8x8 slice. The times are simulated.
512 devices in a mesh: dom: 16 (over z_lo, x, core), band: 32 (over z_hi, y).
Axes of the slice: x: 4, y: 8, z: 8 (z_hi: 4, z_lo: 2; z = z_hi * 2 + z_lo), core: 2. Of those that a mesh axis runs over, the one named last changes fastest.
Arguments:
- orbitals: bfloat16 [1024, 16, 2, 16, 128], P('band', 'dom'), may hold values from -6 to 6
- potential: float32 [16, 2, 16, 128], P('dom'), may hold values from -1 to 1
- ritz: bfloat16 [1024, 1024], P(None, 'band'), may hold values from -0.1875 to 0.1875
Outputs:
- rotated: float32 [1024, 16, 2, 16, 128], P('band', 'dom')
All inputs are finite; a program needn't handle non-finite values.
Results may differ from a plain program's by a relative error of at most 0.0029.
Values may be sent and summed in bfloat16 or wider, within the bound.
No kernel may reach another device: no remote copies, remote signals or barrier semaphores. Data moves between devices by JAX's collectives and lax.ppermute only.
A program may use at most 64 MiB of HBM per device.

v0:
```python
import math
import jax
import jax.numpy as jnp
from jax import lax
from jax.sharding import PartitionSpec as P

DEG = 4
lower_bound = -1.5
cut_off = 1.0
upper_bound = 9.5
coef_zero = -2.5
coef_one = 4.0 / 3.0
coef_two = -1.0 / 12.0


def shifted(value, axis, steps):
    count = lax.axis_size(axis)
    pairs = [(source, (source + steps) % count) for source in range(count)]
    return lax.ppermute(value, axis, pairs)


def filter_weights(degree):
    half_width = (upper_bound - cut_off) / 2.0
    centre = (upper_bound + cut_off) / 2.0
    sigma_now = half_width / (lower_bound - centre)
    first_scale = sigma_now / half_width
    inverse_gain = 2.0 / sigma_now
    weights = []
    for degree_step in range(1, degree):
        sigma_next = 1.0 / (inverse_gain - sigma_now)
        weights.append((2.0 * sigma_next / half_width, sigma_now * sigma_next))
        sigma_now = sigma_next
    return (centre, first_scale, weights)


def send_first(face, offset):
    return shifted(face, "dom", offset)


def send_second(face, offset):
    return shifted(face, "dom", offset)


def padded_second(padded, count, axis):
    lower_near = lax.slice_in_dim(padded, 1, count + 1, axis=axis)
    upper_near = lax.slice_in_dim(padded, 3, count + 3, axis=axis)
    lower_far = lax.slice_in_dim(padded, 0, count, axis=axis)
    upper_far = lax.slice_in_dim(padded, 4, count + 4, axis=axis)
    return coef_one * (lower_near + upper_near) + coef_two * (lower_far + upper_far)


def apply_ham(field_now, local_pot, grid_side, row_y):
    cells_x = field_now.shape[1]
    cells_y = field_now.shape[2]
    low_x = send_first(field_now, grid_side)
    high_x = send_first(field_now, -grid_side)
    along_x = jnp.concatenate([low_x, field_now, high_x], axis=1)
    top_y = field_now[:, :, cells_y - 2 :]
    bottom_y = field_now[:, :, :2]
    low_y = jnp.where(row_y == 0, send_second(top_y, 1 - grid_side), send_second(top_y, 1))
    high_y = jnp.where(
        row_y == grid_side - 1, send_second(bottom_y, grid_side - 1), send_second(bottom_y, -1)
    )
    along_y = jnp.concatenate([low_y, field_now, high_y], axis=2)
    near_z = jnp.roll(field_now, 1, 3) + jnp.roll(field_now, -1, 3)
    far_z = jnp.roll(field_now, 2, 3) + jnp.roll(field_now, -2, 3)
    second = (
        3.0 * coef_zero * field_now
        + padded_second(along_x, cells_x, 1)
        + padded_second(along_y, cells_y, 2)
    )
    second = second + (coef_one * near_z + coef_two * far_z)
    return -0.5 * second + local_pot * field_now


def on_device(orbitals, potential, ritz):
    grid_side = math.isqrt(lax.axis_size("dom"))
    row_y = lax.axis_index("dom") % grid_side
    centre, first_scale, weights = filter_weights(DEG)
    local_pot = potential[0]
    previous = orbitals[:, 0].astype(jnp.float32)
    current = (apply_ham(previous, local_pot, grid_side, row_y) - centre * previous) * first_scale
    for scale_h, scale_x in weights:
        following = (
            apply_ham(current, local_pot, grid_side, row_y) - centre * current
        ) * scale_h - scale_x * previous
        previous, current = (current, following)
    band_rows = current.shape[0]
    flat_panel = current.astype(jnp.bfloat16).reshape(band_rows, -1)
    rotated = lax.dot_general(
        ritz,
        lax.all_gather(flat_panel, "band", axis=0, tiled=True),
        (((0,), (0,)), ((), ())),
        preferred_element_type=jnp.float32,
    )
    return rotated.reshape(orbitals.shape)


def solution(mesh):
    in_specs = (P("band", "dom", None, None, None), P("dom", None, None, None), P(None, "band"))
    out_specs = P("band", "dom", None, None, None)
    return jax.shard_map(
        on_device, mesh=mesh, in_specs=in_specs, out_specs=out_specs, check_vma=False
    )
```

profile of v0, /device:TPU:1, one launch (start us, length us, event | category | flops | bytes accessed | tf_op | source)
XLA Modules:
  0.0 319.9 jit_solution(1605391283668732699)
XLA Ops:
  6.5 1.1 bitcast_convert_fusion
  7.6 0.7 fusion.99
  8.3 4.5 %collective-permute-start.3 = (f32[32,2,2,128]{3,2,1,0:T(2,128)}, f32[32,2,2,128]{3,2,1,0:T(2,128)}, u32[]{:S(2)}, u32[]{:S(2)}) collective-permute-start(f32[32,2,2,128]{3,2,1,0:T(2,128)} %get-tuple-element.37), channel_id=1, source_target_pairs={{0,32},{32,64},{64,96},{96,128},{128,160},{160,192},{192,224},{224... | collective-permute-start | bytes 196616 | tf_op jit(solution)/shard_map/ppermute | solution.py:19
  12.8 5.0 %collective-permute-start.2 = (f32[32,2,2,128]{3,2,1,0:T(2,128)}, f32[32,2,2,128]{3,2,1,0:T(2,128)}, u32[]{:S(2)}, u32[]{:S(2)}) collective-permute-start(f32[32,2,2,128]{3,2,1,0:T(2,128)} %get-tuple-element.37), channel_id=1, source_target_pairs={{0,416},{32,448},{64,480},{96,0},{128,32},{160,64},{192,96},{224,1... | collective-permute-start | bytes 196616 | tf_op jit(solution)/shard_map/ppermute | solution.py:19
  17.8 3.1 collective-permute-start.1
  20.9 3.7 %collective-permute-start = (f32[32,2,16,128]{3,2,1,0:T(8,128)S(1)}, f32[32,2,16,128]{3,2,1,0:T(8,128)}, u32[]{:S(2)}, u32[]{:S(2)}) collective-permute-start(f32[32,2,16,128]{3,2,1,0:T(8,128)S(1)} %bitcast_convert_fusion), channel_id=1, source_target_pairs={{0,128},{32,160},{64,192},{96,224},{128,256},{160,288},{192,320},{... | collective-permute-start | bytes 1572872 | tf_op jit(solution)/shard_map/ppermute | solution.py:19
  24.6 4.0 %collective-permute-start.5 = (f32[32,2,2,128]{3,2,1,0:T(2,128)}, f32[32,2,2,128]{3,2,1,0:T(2,128)}, u32[]{:S(2)}, u32[]{:S(2)}) collective-permute-start(f32[32,2,2,128]{3,2,1,0:T(2,128)} %get-tuple-element.38), channel_id=1, source_target_pairs={{0,480},{32,0},{64,32},{96,64},{128,96},{160,128},{192,160},{224,1... | collective-permute-start | bytes 196616 | tf_op jit(solution)/shard_map/ppermute | solution.py:19
  28.7 0.2 fusion.101
  28.9 0.2 fusion.100
  29.1 1.0 fusion.103
  30.1 1.1 fusion.102
  31.3 0.0 collective-permute-done.3
  31.3 4.4 %collective-permute-start.4 = (f32[32,2,2,128]{3,2,1,0:T(2,128)}, f32[32,2,2,128]{3,2,1,0:T(2,128)S(1)}, u32[]{:S(2)}, u32[]{:S(2)}) collective-permute-start(f32[32,2,2,128]{3,2,1,0:T(2,128)} %get-tuple-element.38), channel_id=1, source_target_pairs={{0,96},{32,128},{64,160},{96,192},{128,224},{160,256},{192,288},{2... | collective-permute-start | bytes 196616 | tf_op jit(solution)/shard_map/ppermute | solution.py:19
  35.7 0.9 broadcast_select_fusion.7
  36.6 10.4 %collective-permute-done.5 = f32[32,2,2,128]{3,2,1,0:T(2,128)} collective-permute-done((f32[32,2,2,128]{3,2,1,0:T(2,128)}, f32[32,2,2,128]{3,2,1,0:T(2,128)}, u32[]{:S(2)}, u32[]{:S(2)}) %collective-permute-start.5) | collective-permute-done | bytes 65568 | tf_op jit(solution)/shard_map/ppermute | solution.py:19
  47.0 0.9 broadcast_select_fusion.3
  47.9 0.0 collective-permute-done
  47.9 2.9 broadcast_multiply_fusion
  50.8 4.1 %collective-permute-start.9 = (f32[32,2,2,128]{3,2,1,0:T(2,128)S(1)}, f32[32,2,2,128]{3,2,1,0:T(2,128)S(1)}, u32[]{:S(2)}, u32[]{:S(2)}) collective-permute-start(f32[32,2,2,128]{3,2,1,0:T(2,128)S(1)} %get-tuple-element.35), channel_id=1, source_target_pairs={{0,32},{32,64},{64,96},{96,128},{128,160},{160,192},{192,224},{224... | collective-permute-start | bytes 196616 | tf_op jit(solution)/shard_map/ppermute | solution.py:19
  54.9 6.9 %collective-permute-start.8 = (f32[32,2,2,128]{3,2,1,0:T(2,128)S(1)}, f32[32,2,2,128]{3,2,1,0:T(2,128)S(1)}, u32[]{:S(2)}, u32[]{:S(2)}) collective-permute-start(f32[32,2,2,128]{3,2,1,0:T(2,128)S(1)} %get-tuple-element.35), channel_id=1, source_target_pairs={{0,416},{32,448},{64,480},{96,0},{128,32},{160,64},{192,96},{224,1... | collective-permute-start | bytes 196616 | tf_op jit(solution)/shard_map/ppermute | solution.py:19
  61.9 3.1 collective-permute-start.7
  65.0 3.7 %collective-permute-start.6 = (f32[32,2,16,128]{3,2,1,0:T(8,128)S(1)}, f32[32,2,16,128]{3,2,1,0:T(8,128)S(1)}, u32[]{:S(2)}, u32[]{:S(2)}) collective-permute-start(f32[32,2,16,128]{3,2,1,0:T(8,128)S(1)} %get-tuple-element.5), channel_id=1, source_target_pairs={{0,128},{32,160},{64,192},{96,224},{128,256},{160,288},{192,320},{... | collective-permute-start | bytes 1572872 | tf_op jit(solution)/shard_map/ppermute | solution.py:19
  68.7 0.2 fusion.96
  68.9 0.2 fusion.94
  69.1 0.2 fusion.95
  69.3 0.2 fusion.97
  69.5 4.0 %collective-permute-start.11 = (f32[32,2,2,128]{3,2,1,0:T(2,128)S(1)}, f32[32,2,2,128]{3,2,1,0:T(2,128)S(1)}, u32[]{:S(2)}, u32[]{:S(2)}) collective-permute-start(f32[32,2,2,128]{3,2,1,0:T(2,128)S(1)} %get-tuple-element.36), channel_id=1, source_target_pairs={{0,480},{32,0},{64,32},{96,64},{128,96},{160,128},{192,160},{224,1... | collective-permute-start | bytes 196616 | tf_op jit(solution)/shard_map/ppermute | solution.py:19
  73.6 1.9 collective-permute-start.10
  75.5 0.0 collective-permute-done.8
  75.6 13.0 %collective-permute-done.11 = f32[32,2,2,128]{3,2,1,0:T(2,128)S(1)} collective-permute-done((f32[32,2,2,128]{3,2,1,0:T(2,128)S(1)}, f32[32,2,2,128]{3,2,1,0:T(2,128)S(1)}, u32[]{:S(2)}, u32[]{:S(2)}) %collective-permute-start.11) | collective-permute-done | bytes 65568 | tf_op jit(solution)/shard_map/ppermute | solution.py:19
  88.6 0.0 collective-permute-done.10
  88.6 1.1 collective-permute-done.7
  89.8 1.1 fusion.34
  90.9 1.9 collective-permute-start.15
  92.8 4.1 %collective-permute-start.14 = (f32[32,2,2,128]{3,2,1,0:T(2,128)S(1)}, f32[32,2,2,128]{3,2,1,0:T(2,128)S(1)}, u32[]{:S(2)}, u32[]{:S(2)}) collective-permute-start(f32[32,2,2,128]{3,2,1,0:T(2,128)S(1)} %get-tuple-element.25), channel_id=1, source_target_pairs={{0,416},{32,448},{64,480},{96,0},{128,32},{160,64},{192,96},{224,1... | collective-permute-start | bytes 196616 | tf_op jit(solution)/shard_map/ppermute | solution.py:19
  96.9 4.4 %collective-permute-start.13 = (f32[32,2,16,128]{3,2,1,0:T(8,128)S(1)}, f32[32,2,16,128]{3,2,1,0:T(8,128)S(1)}, u32[]{:S(2)}, u32[]{:S(2)}) collective-permute-start(f32[32,2,16,128]{3,2,1,0:T(8,128)S(1)} %fusion.34), channel_id=1, source_target_pairs={{0,384},{32,416},{64,448},{96,480},{128,0},{160,32},{192,64},{224,... | collective-permute-start | bytes 1572872 | tf_op jit(solution)/shard_map/ppermute | solution.py:19
  101.3 2.4 collective-permute-start.12
  103.8 0.2 fusion.91
  104.0 0.2 fusion.90
  104.2 0.2 fusion.89
  104.4 0.2 fusion.92
  104.6 4.9 %collective-permute-start.17 = (f32[32,2,2,128]{3,2,1,0:T(2,128)S(1)}, f32[32,2,2,128]{3,2,1,0:T(2,128)S(1)}, u32[]{:S(2)}, u32[]{:S(2)}) collective-permute-start(f32[32,2,2,128]{3,2,1,0:T(2,128)S(1)} %get-tuple-element.26), channel_id=1, source_target_pairs={{0,480},{32,0},{64,32},{96,64},{128,96},{160,128},{192,160},{224,1... | collective-permute-start | bytes 196616 | tf_op jit(solution)/shard_map/ppermute | solution.py:19
  109.5 0.0 collective-permute-done.15
  109.5 2.6 collective-permute-start.16
  112.2 0.0 collective-permute-done.14
  112.2 14.9 %collective-permute-done.17 = f32[32,2,2,128]{3,2,1,0:T(2,128)S(1)} collective-permute-done((f32[32,2,2,128]{3,2,1,0:T(2,128)S(1)}, f32[32,2,2,128]{3,2,1,0:T(2,128)S(1)}, u32[]{:S(2)}, u32[]{:S(2)}) %collective-permute-start.17) | collective-permute-done | bytes 65568 | tf_op jit(solution)/shard_map/ppermute | solution.py:19
  127.2 1.0 fusion.22
  128.3 2.9 collective-permute-start.21
  131.2 6.1 %collective-permute-start.20 = (f32[32,2,2,128]{3,2,1,0:T(2,128)S(1)}, f32[32,2,2,128]{3,2,1,0:T(2,128)S(1)}, u32[]{:S(2)}, u32[]{:S(2)}) collective-permute-start(f32[32,2,2,128]{3,2,1,0:T(2,128)S(1)} %get-tuple-element.7), channel_id=1, source_target_pairs={{0,416},{32,448},{64,480},{96,0},{128,32},{160,64},{192,96},{224,1... | collective-permute-start | bytes 196616 | tf_op jit(solution)/shard_map/ppermute | solution.py:19
  137.4 3.1 collective-permute-start.19
  140.5 3.7 %collective-permute-start.18 = (f32[32,2,16,128]{3,2,1,0:T(8,128)S(1)}, f32[32,2,16,128]{3,2,1,0:T(8,128)S(1)}, u32[]{:S(2)}, u32[]{:S(2)}) collective-permute-start(f32[32,2,16,128]{3,2,1,0:T(8,128)S(1)} %fusion.22), channel_id=1, source_target_pairs={{0,128},{32,160},{64,192},{96,224},{128,256},{160,288},{192,320},{... | collective-permute-start | bytes 1572872 | tf_op jit(solution)/shard_map/ppermute | solution.py:19
  144.2 0.2 fusion.88
  144.4 0.2 fusion.85
  144.6 0.2 fusion.86
  144.8 0.2 fusion.87
  145.0 4.0 %collective-permute-start.23 = (f32[32,2,2,128]{3,2,1,0:T(2,128)S(1)}, f32[32,2,2,128]{3,2,1,0:T(2,128)S(1)}, u32[]{:S(2)}, u32[]{:S(2)}) collective-permute-start(f32[32,2,2,128]{3,2,1,0:T(2,128)S(1)} %get-tuple-element.8), channel_id=1, source_target_pairs={{0,480},{32,0},{64,32},{96,64},{128,96},{160,128},{192,160},{224,1... | collective-permute-start | bytes 196616 | tf_op jit(solution)/shard_map/ppermute | solution.py:19
  149.1 1.9 collective-permute-start.22
  151.1 14.7 %collective-permute-done.23 = f32[32,2,2,128]{3,2,1,0:T(2,128)S(1)} collective-permute-done((f32[32,2,2,128]{3,2,1,0:T(2,128)S(1)}, f32[32,2,2,128]{3,2,1,0:T(2,128)S(1)}, u32[]{:S(2)}, u32[]{:S(2)}) %collective-permute-start.23) | collective-permute-done | bytes 65568 | tf_op jit(solution)/shard_map/ppermute | solution.py:19
  165.9 1.0 fusion.82
  166.9 0.8 copy.8
  167.7 0.0 all-gather.2.cloned.1.call-update
  167.8 139.5 %all-gather.2.cloned.1.call-done = bf16[1024,4096]{1,0:T(8,128)(2,1)} async-done(((bf16[32,4096]{1,0:T(8,128)(2,1)}), bf16[1024,4096]{1,0:T(8,128)(2,1)}) %all-gather.2.cloned.1.call-update) | async-done | bytes 8388624 | tf_op jit(solution)/shard_map/all_gather | solution.py:92
  307.2 4.9 %convolution_bitcast_fusion = f32[4,8,32,128]{3,1,2,0:T(8,128)S(1)} fusion(bf16[1024,32]{0,1:T(8,128)(2,1)S(1)} %copy-done, bf16[1024,4096]{1,0:T(8,128)(2,1)} %all-gather.2.cloned.1.call-done), kind=kOutput, calls=%fused_computation | convolution fusion | flops 268435456 | bytes 8978432 | tf_op jit(solution)/shard_map/dot_general | solution.py:90
  312.2 0.9 copy.6
  (30 shorter events, 0.4 us)
Async XLA Ops:
  6.5 300.7 %copy-start = (bf16[1024,32]{0,1:T(8,128)(2,1)S(1)}, bf16[1024,32]{0,1:T(8,128)(2,1)}, u32[]{:S(2)}) copy-start(bf16[1024,32]{0,1:T(8,128)(2,1)} %param.5) | copy-start | bytes 196612
  6.5 41.4 %copy-start.1 = (bf16[32,1,2,16,128]{4,3,2,1,0:T(8,128)(2,1)S(1)}, bf16[32,1,2,16,128]{4,3,2,1,0:T(8,128)(2,1)}, u32[]{:S(2)}) copy-start(bf16[32,1,2,16,128]{4,3,2,1,0:T(8,128)(2,1)} %param.3) | copy-start | bytes 786436
  6.5 24.7 %copy-start.2 = (f32[1,2,16,128]{3,2,1,0:T(8,128)S(1)}, f32[1,2,16,128]{3,2,1,0:T(8,128)}, u32[]{:S(2)}) copy-start(f32[1,2,16,128]{3,2,1,0:T(8,128)} %param.4) | copy-start | bytes 49156
  6.5 300.7 %all-gather.2.cloned.1.call-start = ((), (), s32[]{:S(2)}) async-start(), calls=%async_computation | async-start | bytes 8650752 | tf_op jit(solution)/shard_map/all_gather | solution.py:92
  8.3 22.9 %collective-permute-start.3 = (f32[32,2,2,128]{3,2,1,0:T(2,128)}, f32[32,2,2,128]{3,2,1,0:T(2,128)}, u32[]{:S(2)}, u32[]{:S(2)}) collective-permute-start(f32[32,2,2,128]{3,2,1,0:T(2,128)} %get-tuple-element.37), channel_id=1, source_target_pairs={{0,32},{32,64},{64,96},{96,128},{128,160},{160,192},{192,224},{224... | collective-permute-start | bytes 196616 | tf_op jit(solution)/shard_map/ppermute | solution.py:19
  12.8 22.8 %collective-permute-start.2 = (f32[32,2,2,128]{3,2,1,0:T(2,128)}, f32[32,2,2,128]{3,2,1,0:T(2,128)}, u32[]{:S(2)}, u32[]{:S(2)}) collective-permute-start(f32[32,2,2,128]{3,2,1,0:T(2,128)} %get-tuple-element.37), channel_id=1, source_target_pairs={{0,416},{32,448},{64,480},{96,0},{128,32},{160,64},{192,96},{224,1... | collective-permute-start | bytes 196616 | tf_op jit(solution)/shard_map/ppermute | solution.py:19
  17.8 30.1 %collective-permute-start.1 = (f32[32,2,16,128]{3,2,1,0:T(8,128)S(1)}, f32[32,2,16,128]{3,2,1,0:T(8,128)}, u32[]{:S(2)}, u32[]{:S(2)}) collective-permute-start(f32[32,2,16,128]{3,2,1,0:T(8,128)S(1)} %bitcast_convert_fusion), channel_id=1, source_target_pairs={{0,384},{32,416},{64,448},{96,480},{128,0},{160,32},{192,64},{224,... | collective-permute-start | bytes 1572872 | tf_op jit(solution)/shard_map/ppermute | solution.py:19
  20.9 27.0 %collective-permute-start = (f32[32,2,16,128]{3,2,1,0:T(8,128)S(1)}, f32[32,2,16,128]{3,2,1,0:T(8,128)}, u32[]{:S(2)}, u32[]{:S(2)}) collective-permute-start(f32[32,2,16,128]{3,2,1,0:T(8,128)S(1)} %bitcast_convert_fusion), channel_id=1, source_target_pairs={{0,128},{32,160},{64,192},{96,224},{128,256},{160,288},{192,320},{... | collective-permute-start | bytes 1572872 | tf_op jit(solution)/shard_map/ppermute | solution.py:19
  24.6 22.4 %collective-permute-start.5 = (f32[32,2,2,128]{3,2,1,0:T(2,128)}, f32[32,2,2,128]{3,2,1,0:T(2,128)}, u32[]{:S(2)}, u32[]{:S(2)}) collective-permute-start(f32[32,2,2,128]{3,2,1,0:T(2,128)} %get-tuple-element.38), channel_id=1, source_target_pairs={{0,480},{32,0},{64,32},{96,64},{128,96},{160,128},{192,160},{224,1... | collective-permute-start | bytes 196616 | tf_op jit(solution)/shard_map/ppermute | solution.py:19
  31.3 15.7 %collective-permute-start.4 = (f32[32,2,2,128]{3,2,1,0:T(2,128)}, f32[32,2,2,128]{3,2,1,0:T(2,128)S(1)}, u32[]{:S(2)}, u32[]{:S(2)}) collective-permute-start(f32[32,2,2,128]{3,2,1,0:T(2,128)} %get-tuple-element.38), channel_id=1, source_target_pairs={{0,96},{32,128},{64,160},{96,192},{128,224},{160,256},{192,288},{2... | collective-permute-start | bytes 196616 | tf_op jit(solution)/shard_map/ppermute | solution.py:19
  50.8 22.7 %collective-permute-start.9 = (f32[32,2,2,128]{3,2,1,0:T(2,128)S(1)}, f32[32,2,2,128]{3,2,1,0:T(2,128)S(1)}, u32[]{:S(2)}, u32[]{:S(2)}) collective-permute-start(f32[32,2,2,128]{3,2,1,0:T(2,128)S(1)} %get-tuple-element.35), channel_id=1, source_target_pairs={{0,32},{32,64},{64,96},{96,128},{128,160},{160,192},{192,224},{224... | collective-permute-start | bytes 196616 | tf_op jit(solution)/shard_map/ppermute | solution.py:19
  54.9 20.6 %collective-permute-start.8 = (f32[32,2,2,128]{3,2,1,0:T(2,128)S(1)}, f32[32,2,2,128]{3,2,1,0:T(2,128)S(1)}, u32[]{:S(2)}, u32[]{:S(2)}) collective-permute-start(f32[32,2,2,128]{3,2,1,0:T(2,128)S(1)} %get-tuple-element.35), channel_id=1, source_target_pairs={{0,416},{32,448},{64,480},{96,0},{128,32},{160,64},{192,96},{224,1... | collective-permute-start | bytes 196616 | tf_op jit(solution)/shard_map/ppermute | solution.py:19
  61.9 27.9 %collective-permute-start.7 = (f32[32,2,16,128]{3,2,1,0:T(8,128)S(1)}, f32[32,2,16,128]{3,2,1,0:T(8,128)S(1)}, u32[]{:S(2)}, u32[]{:S(2)}) collective-permute-start(f32[32,2,16,128]{3,2,1,0:T(8,128)S(1)} %get-tuple-element.5), channel_id=1, source_target_pairs={{0,384},{32,416},{64,448},{96,480},{128,0},{160,32},{192,64},{224,... | collective-permute-start | bytes 1572872 | tf_op jit(solution)/shard_map/ppermute | solution.py:19
  65.0 24.8 %collective-permute-start.6 = (f32[32,2,16,128]{3,2,1,0:T(8,128)S(1)}, f32[32,2,16,128]{3,2,1,0:T(8,128)S(1)}, u32[]{:S(2)}, u32[]{:S(2)}) collective-permute-start(f32[32,2,16,128]{3,2,1,0:T(8,128)S(1)} %get-tuple-element.5), channel_id=1, source_target_pairs={{0,128},{32,160},{64,192},{96,224},{128,256},{160,288},{192,320},{... | collective-permute-start | bytes 1572872 | tf_op jit(solution)/shard_map/ppermute | solution.py:19
  69.5 19.1 %collective-permute-start.11 = (f32[32,2,2,128]{3,2,1,0:T(2,128)S(1)}, f32[32,2,2,128]{3,2,1,0:T(2,128)S(1)}, u32[]{:S(2)}, u32[]{:S(2)}) collective-permute-start(f32[32,2,2,128]{3,2,1,0:T(2,128)S(1)} %get-tuple-element.36), channel_id=1, source_target_pairs={{0,480},{32,0},{64,32},{96,64},{128,96},{160,128},{192,160},{224,1... | collective-permute-start | bytes 196616 | tf_op jit(solution)/shard_map/ppermute | solution.py:19
  73.6 15.0 %collective-permute-start.10 = (f32[32,2,2,128]{3,2,1,0:T(2,128)S(1)}, f32[32,2,2,128]{3,2,1,0:T(2,128)S(1)}, u32[]{:S(2)}, u32[]{:S(2)}) collective-permute-start(f32[32,2,2,128]{3,2,1,0:T(2,128)S(1)} %get-tuple-element.36), channel_id=1, source_target_pairs={{0,96},{32,128},{64,160},{96,192},{128,224},{160,256},{192,288},{2... | collective-permute-start | bytes 196616 | tf_op jit(solution)/shard_map/ppermute | solution.py:19
  90.9 18.6 %collective-permute-start.15 = (f32[32,2,2,128]{3,2,1,0:T(2,128)S(1)}, f32[32,2,2,128]{3,2,1,0:T(2,128)S(1)}, u32[]{:S(2)}, u32[]{:S(2)}) collective-permute-start(f32[32,2,2,128]{3,2,1,0:T(2,128)S(1)} %get-tuple-element.25), channel_id=1, source_target_pairs={{0,32},{32,64},{64,96},{96,128},{128,160},{160,192},{192,224},{224... | collective-permute-start | bytes 196616 | tf_op jit(solution)/shard_map/ppermute | solution.py:19
  92.8 19.3 %collective-permute-start.14 = (f32[32,2,2,128]{3,2,1,0:T(2,128)S(1)}, f32[32,2,2,128]{3,2,1,0:T(2,128)S(1)}, u32[]{:S(2)}, u32[]{:S(2)}) collective-permute-start(f32[32,2,2,128]{3,2,1,0:T(2,128)S(1)} %get-tuple-element.25), channel_id=1, source_target_pairs={{0,416},{32,448},{64,480},{96,0},{128,32},{160,64},{192,96},{224,1... | collective-permute-start | bytes 196616 | tf_op jit(solution)/shard_map/ppermute | solution.py:19
  96.9 30.2 %collective-permute-start.13 = (f32[32,2,16,128]{3,2,1,0:T(8,128)S(1)}, f32[32,2,16,128]{3,2,1,0:T(8,128)S(1)}, u32[]{:S(2)}, u32[]{:S(2)}) collective-permute-start(f32[32,2,16,128]{3,2,1,0:T(8,128)S(1)} %fusion.34), channel_id=1, source_target_pairs={{0,384},{32,416},{64,448},{96,480},{128,0},{160,32},{192,64},{224,... | collective-permute-start | bytes 1572872 | tf_op jit(solution)/shard_map/ppermute | solution.py:19
  101.3 25.9 %collective-permute-start.12 = (f32[32,2,16,128]{3,2,1,0:T(8,128)S(1)}, f32[32,2,16,128]{3,2,1,0:T(8,128)S(1)}, u32[]{:S(2)}, u32[]{:S(2)}) collective-permute-start(f32[32,2,16,128]{3,2,1,0:T(8,128)S(1)} %fusion.34), channel_id=1, source_target_pairs={{0,128},{32,160},{64,192},{96,224},{128,256},{160,288},{192,320},{... | collective-permute-start | bytes 1572872 | tf_op jit(solution)/shard_map/ppermute | solution.py:19
  104.6 22.6 %collective-permute-start.17 = (f32[32,2,2,128]{3,2,1,0:T(2,128)S(1)}, f32[32,2,2,128]{3,2,1,0:T(2,128)S(1)}, u32[]{:S(2)}, u32[]{:S(2)}) collective-permute-start(f32[32,2,2,128]{3,2,1,0:T(2,128)S(1)} %get-tuple-element.26), channel_id=1, source_target_pairs={{0,480},{32,0},{64,32},{96,64},{128,96},{160,128},{192,160},{224,1... | collective-permute-start | bytes 196616 | tf_op jit(solution)/shard_map/ppermute | solution.py:19
  109.5 17.6 %collective-permute-start.16 = (f32[32,2,2,128]{3,2,1,0:T(2,128)S(1)}, f32[32,2,2,128]{3,2,1,0:T(2,128)S(1)}, u32[]{:S(2)}, u32[]{:S(2)}) collective-permute-start(f32[32,2,2,128]{3,2,1,0:T(2,128)S(1)} %get-tuple-element.26), channel_id=1, source_target_pairs={{0,96},{32,128},{64,160},{96,192},{128,224},{160,256},{192,288},{2... | collective-permute-start | bytes 196616 | tf_op jit(solution)/shard_map/ppermute | solution.py:19
  128.3 20.8 %collective-permute-start.21 = (f32[32,2,2,128]{3,2,1,0:T(2,128)S(1)}, f32[32,2,2,128]{3,2,1,0:T(2,128)S(1)}, u32[]{:S(2)}, u32[]{:S(2)}) collective-permute-start(f32[32,2,2,128]{3,2,1,0:T(2,128)S(1)} %get-tuple-element.7), channel_id=1, source_target_pairs={{0,32},{32,64},{64,96},{96,128},{128,160},{160,192},{192,224},{224... | collective-permute-start | bytes 196616 | tf_op jit(solution)/shard_map/ppermute | solution.py:19
  131.2 19.8 %collective-permute-start.20 = (f32[32,2,2,128]{3,2,1,0:T(2,128)S(1)}, f32[32,2,2,128]{3,2,1,0:T(2,128)S(1)}, u32[]{:S(2)}, u32[]{:S(2)}) collective-permute-start(f32[32,2,2,128]{3,2,1,0:T(2,128)S(1)} %get-tuple-element.7), channel_id=1, source_target_pairs={{0,416},{32,448},{64,480},{96,0},{128,32},{160,64},{192,96},{224,1... | collective-permute-start | bytes 196616 | tf_op jit(solution)/shard_map/ppermute | solution.py:19
  137.4 28.5 %collective-permute-start.19 = (f32[32,2,16,128]{3,2,1,0:T(8,128)S(1)}, f32[32,2,16,128]{3,2,1,0:T(8,128)S(1)}, u32[]{:S(2)}, u32[]{:S(2)}) collective-permute-start(f32[32,2,16,128]{3,2,1,0:T(8,128)S(1)} %fusion.22), channel_id=1, source_target_pairs={{0,384},{32,416},{64,448},{96,480},{128,0},{160,32},{192,64},{224,... | collective-permute-start | bytes 1572872 | tf_op jit(solution)/shard_map/ppermute | solution.py:19
  140.5 25.4 %collective-permute-start.18 = (f32[32,2,16,128]{3,2,1,0:T(8,128)S(1)}, f32[32,2,16,128]{3,2,1,0:T(8,128)S(1)}, u32[]{:S(2)}, u32[]{:S(2)}) collective-permute-start(f32[32,2,16,128]{3,2,1,0:T(8,128)S(1)} %fusion.22), channel_id=1, source_target_pairs={{0,128},{32,160},{64,192},{96,224},{128,256},{160,288},{192,320},{... | collective-permute-start | bytes 1572872 | tf_op jit(solution)/shard_map/ppermute | solution.py:19
  145.0 20.8 %collective-permute-start.23 = (f32[32,2,2,128]{3,2,1,0:T(2,128)S(1)}, f32[32,2,2,128]{3,2,1,0:T(2,128)S(1)}, u32[]{:S(2)}, u32[]{:S(2)}) collective-permute-start(f32[32,2,2,128]{3,2,1,0:T(2,128)S(1)} %get-tuple-element.8), channel_id=1, source_target_pairs={{0,480},{32,0},{64,32},{96,64},{128,96},{160,128},{192,160},{224,1... | collective-permute-start | bytes 196616 | tf_op jit(solution)/shard_map/ppermute | solution.py:19
  149.1 16.7 %collective-permute-start.22 = (f32[32,2,2,128]{3,2,1,0:T(2,128)S(1)}, f32[32,2,2,128]{3,2,1,0:T(2,128)S(1)}, u32[]{:S(2)}, u32[]{:S(2)}) collective-permute-start(f32[32,2,2,128]{3,2,1,0:T(2,128)S(1)} %get-tuple-element.8), channel_id=1, source_target_pairs={{0,96},{32,128},{64,160},{96,192},{128,224},{160,256},{192,288},{2... | collective-permute-start | bytes 196616 | tf_op jit(solution)/shard_map/ppermute | solution.py:19
Sparse Core Ops, SparseCore 0:
  167.9 139.3 all-gather.1
where the time goes:
time: 321 us; the launch traced here: 320 us
  waiting for transfers between devices  194 us (60%)
  starting transfers between devices  90.6 us (28%)
  between operations  13.8 us (4%)
  other arithmetic  9.05 us (3%)
  local copies, waits for them, and re-layouts  7.66 us (2%)
  matrix products  4.92 us (2%)
    all_gather x1, waiting for transfers between devices, on_device(): lax.all_gather(flat_panel, 'band', axis=0, tiled=True)  139 us
    ppermute x24, starting transfers between devices, shifted(): return lax.ppermute(value, axis, pairs)  90.6 us
    ppermute x24, waiting for transfers between devices, shifted(): return lax.ppermute(value, axis, pairs)  54.3 us
  transfers between devices with their start and end apart: 25, of which 6 were waited for; matrix products, arithmetic and copies ran while one was open for 2% of the time, Pallas kernels for 0%

commit v1 on v0

--- a/solution.py
+++ b/solution.py
@@ -1,3 +1,4 @@
+import functools
 import math
 import jax
 import jax.numpy as jnp
@@ -11,6 +12,21 @@
 coef_zero = -2.5
 coef_one = 4.0 / 3.0
 coef_two = -1.0 / 12.0
+
+
+def cover_the_groups(mine, lane_axis):
+    return jnp.concatenate(
+        lax.all_to_all(
+            jnp.stack([mine for _ in range(lax.psum(1, axis_name=lane_axis))]),
+            lane_axis,
+            split_axis=0,
+            concat_axis=0,
+        ),
+        axis=0,
+    )
+
+
+_convert_values = functools.partial(cover_the_groups, lane_axis="band")
 
 
 def shifted(value, axis, steps):
@@ -89,7 +105,7 @@
     flat_panel = current.astype(jnp.bfloat16).reshape(band_rows, -1)
     rotated = lax.dot_general(
         ritz,
-        lax.all_gather(flat_panel, "band", axis=0, tiled=True),
+        _convert_values(flat_panel),
         (((0,), (0,)), ((), ())),
         preferred_element_type=jnp.float32,
     )

time: 321 us -> 386 us (1.20)
  the two profiles are of different devices: /device:TPU:1 before, /device:TPU:91 now
where the time goes in v1:
time: 386 us; the launch traced here: 385 us
  blocking collectives  227 us (59%)
  starting transfers between devices  84.1 us (22%)
  waiting for transfers between devices  55.5 us (14%)
  other arithmetic  8.23 us (2%)
  local copies, waits for them, and re-layouts  7.99 us (2%)
    all_to_all x1, blocking collectives, cover_the_groups(): lax.all_to_all(jnp.stack([mine for _ in range(lax.psum(1, axis_name=lane_...  227 us
    ppermute x24, starting transfers between devices, shifted(): return lax.ppermute(value, axis, pairs)  84.1 us
    ppermute x24, waiting for transfers between devices, shifted(): return lax.ppermute(value, axis, pairs)  55.5 us
  transfers between devices with their start and end apart: 24, of which 8 were waited for; matrix products, arithmetic and copies ran while one was open for 2% of the time, Pallas kernels for 0%

profile of v1, /device:TPU:91, one launch (start us, length us, event | category | flops | bytes accessed | tf_op | source)
XLA Modules:
  0.0 384.9 jit_solution(3895674172984278480)
XLA Ops:
  0.0 1.1 bitcast_convert_fusion
  1.1 0.7 fusion.99
  1.8 3.7 collective-permute-start.3
  5.5 1.9 collective-permute-start.2
  7.4 3.6 collective-permute-start.1
  11.0 3.1 collective-permute-start
  14.2 4.6 %collective-permute-start.5 = (f32[32,2,2,128]{3,2,1,0:T(2,128)}, f32[32,2,2,128]{3,2,1,0:T(2,128)}, u32[]{:S(2)}, u32[]{:S(2)}) collective-permute-start(f32[32,2,2,128]{3,2,1,0:T(2,128)} %get-tuple-element.38), channel_id=1, source_target_pairs={{0,480},{32,0},{64,32},{96,64},{128,96},{160,128},{192,160},{224,1... | collective-permute-start | bytes 196616 | tf_op jit(solution)/shard_map/ppermute | solution.py:35
  18.8 0.2 fusion.101
  19.0 0.2 fusion.100
  19.2 1.0 fusion.103
  20.2 1.1 fusion.102
  21.4 3.9 %collective-permute-start.4 = (f32[32,2,2,128]{3,2,1,0:T(2,128)}, f32[32,2,2,128]{3,2,1,0:T(2,128)S(1)}, u32[]{:S(2)}, u32[]{:S(2)}) collective-permute-start(f32[32,2,2,128]{3,2,1,0:T(2,128)} %get-tuple-element.38), channel_id=1, source_target_pairs={{0,96},{32,128},{64,160},{96,192},{128,224},{160,256},{192,288},{2... | collective-permute-start | bytes 196616 | tf_op jit(solution)/shard_map/ppermute | solution.py:35
  25.3 0.0 collective-permute-done.2
  25.3 0.9 broadcast_select_fusion.7
  26.2 10.9 %collective-permute-done.5 = f32[32,2,2,128]{3,2,1,0:T(2,128)} collective-permute-done((f32[32,2,2,128]{3,2,1,0:T(2,128)}, f32[32,2,2,128]{3,2,1,0:T(2,128)}, u32[]{:S(2)}, u32[]{:S(2)}) %collective-permute-start.5) | collective-permute-done | bytes 65568 | tf_op jit(solution)/shard_map/ppermute | solution.py:35
  37.2 0.6 collective-permute-done.4
  37.8 0.0 collective-permute-done.1
  37.8 2.9 broadcast_multiply_fusion
  40.7 4.4 %collective-permute-start.9 = (f32[32,2,2,128]{3,2,1,0:T(2,128)S(1)}, f32[32,2,2,128]{3,2,1,0:T(2,128)S(1)}, u32[]{:S(2)}, u32[]{:S(2)}) collective-permute-start(f32[32,2,2,128]{3,2,1,0:T(2,128)S(1)} %get-tuple-element.35), channel_id=1, source_target_pairs={{0,32},{32,64},{64,96},{96,128},{128,160},{160,192},{192,224},{224... | collective-permute-start | bytes 196616 | tf_op jit(solution)/shard_map/ppermute | solution.py:35
  45.1 1.9 collective-permute-start.8
  47.1 2.9 collective-permute-start.7
  50.0 3.9 %collective-permute-start.6 = (f32[32,2,16,128]{3,2,1,0:T(8,128)S(1)}, f32[32,2,16,128]{3,2,1,0:T(8,128)S(1)}, u32[]{:S(2)}, u32[]{:S(2)}) collective-permute-start(f32[32,2,16,128]{3,2,1,0:T(8,128)S(1)} %get-tuple-element.5), channel_id=1, source_target_pairs={{0,128},{32,160},{64,192},{96,224},{128,256},{160,288},{192,320},{... | collective-permute-start | bytes 1572872 | tf_op jit(solution)/shard_map/ppermute | solution.py:35
  53.9 0.2 fusion.96
  54.1 0.2 fusion.94
  54.3 0.2 fusion.95
  54.5 0.2 fusion.97
  54.7 3.8 collective-permute-start.11
  58.6 4.7 %collective-permute-start.10 = (f32[32,2,2,128]{3,2,1,0:T(2,128)S(1)}, f32[32,2,2,128]{3,2,1,0:T(2,128)S(1)}, u32[]{:S(2)}, u32[]{:S(2)}) collective-permute-start(f32[32,2,2,128]{3,2,1,0:T(2,128)S(1)} %get-tuple-element.36), channel_id=1, source_target_pairs={{0,96},{32,128},{64,160},{96,192},{128,224},{160,256},{192,288},{2... | collective-permute-start | bytes 196616 | tf_op jit(solution)/shard_map/ppermute | solution.py:35
  63.3 13.4 %collective-permute-done.11 = f32[32,2,2,128]{3,2,1,0:T(2,128)S(1)} collective-permute-done((f32[32,2,2,128]{3,2,1,0:T(2,128)S(1)}, f32[32,2,2,128]{3,2,1,0:T(2,128)S(1)}, u32[]{:S(2)}, u32[]{:S(2)}) %collective-permute-start.11) | collective-permute-done | bytes 65568 | tf_op jit(solution)/shard_map/ppermute | solution.py:35
  76.8 0.9 collective-permute-done.10
  77.7 0.0 collective-permute-done.7
  77.7 0.0 collective-permute-done.6
  77.7 1.1 fusion.34
  78.9 3.6 collective-permute-start.15
  82.4 2.2 collective-permute-start.14
  84.6 4.6 %collective-permute-start.13 = (f32[32,2,16,128]{3,2,1,0:T(8,128)S(1)}, f32[32,2,16,128]{3,2,1,0:T(8,128)S(1)}, u32[]{:S(2)}, u32[]{:S(2)}) collective-permute-start(f32[32,2,16,128]{3,2,1,0:T(8,128)S(1)} %fusion.34), channel_id=1, source_target_pairs={{0,384},{32,416},{64,448},{96,480},{128,0},{160,32},{192,64},{224,... | collective-permute-start | bytes 1572872 | tf_op jit(solution)/shard_map/ppermute | solution.py:35
  89.2 2.2 collective-permute-start.12
  91.4 0.2 fusion.91
  91.6 0.2 fusion.90
  91.8 0.2 fusion.89
  92.1 0.2 fusion.92
  92.3 5.5 %collective-permute-start.17 = (f32[32,2,2,128]{3,2,1,0:T(2,128)S(1)}, f32[32,2,2,128]{3,2,1,0:T(2,128)S(1)}, u32[]{:S(2)}, u32[]{:S(2)}) collective-permute-start(f32[32,2,2,128]{3,2,1,0:T(2,128)S(1)} %get-tuple-element.26), channel_id=1, source_target_pairs={{0,480},{32,0},{64,32},{96,64},{128,96},{160,128},{192,160},{224,1... | collective-permute-start | bytes 196616 | tf_op jit(solution)/shard_map/ppermute | solution.py:35
  97.8 2.7 collective-permute-start.16
  100.6 13.7 %collective-permute-done.17 = f32[32,2,2,128]{3,2,1,0:T(2,128)S(1)} collective-permute-done((f32[32,2,2,128]{3,2,1,0:T(2,128)S(1)}, f32[32,2,2,128]{3,2,1,0:T(2,128)S(1)}, u32[]{:S(2)}, u32[]{:S(2)}) %collective-permute-start.17) | collective-permute-done | bytes 65568 | tf_op jit(solution)/shard_map/ppermute | solution.py:35
  114.3 0.9 collective-permute-done.16
  115.2 1.0 fusion.22
  116.3 3.6 collective-permute-start.21
  119.9 1.9 collective-permute-start.20
  121.9 3.7 collective-permute-start.19
  125.6 3.1 collective-permute-start.18
  128.7 0.2 fusion.88
  128.9 0.2 fusion.85
  129.1 0.2 fusion.86
  129.3 0.2 fusion.87
  129.5 4.7 %collective-permute-start.23 = (f32[32,2,2,128]{3,2,1,0:T(2,128)S(1)}, f32[32,2,2,128]{3,2,1,0:T(2,128)S(1)}, u32[]{:S(2)}, u32[]{:S(2)}) collective-permute-start(f32[32,2,2,128]{3,2,1,0:T(2,128)S(1)} %get-tuple-element.8), channel_id=1, source_target_pairs={{0,480},{32,0},{64,32},{96,64},{128,96},{160,128},{192,160},{224,1... | collective-permute-start | bytes 196616 | tf_op jit(solution)/shard_map/ppermute | solution.py:35
  134.2 3.9 %collective-permute-start.22 = (f32[32,2,2,128]{3,2,1,0:T(2,128)S(1)}, f32[32,2,2,128]{3,2,1,0:T(2,128)S(1)}, u32[]{:S(2)}, u32[]{:S(2)}) collective-permute-start(f32[32,2,2,128]{3,2,1,0:T(2,128)S(1)} %get-tuple-element.8), channel_id=1, source_target_pairs={{0,96},{32,128},{64,160},{96,192},{128,224},{160,256},{192,288},{2... | collective-permute-start | bytes 196616 | tf_op jit(solution)/shard_map/ppermute | solution.py:35
  138.1 13.4 %collective-permute-done.23 = f32[32,2,2,128]{3,2,1,0:T(2,128)S(1)} collective-permute-done((f32[32,2,2,128]{3,2,1,0:T(2,128)S(1)}, f32[32,2,2,128]{3,2,1,0:T(2,128)S(1)}, u32[]{:S(2)}, u32[]{:S(2)}) %collective-permute-start.23) | collective-permute-done | bytes 65568 | tf_op jit(solution)/shard_map/ppermute | solution.py:35
  151.6 1.6 collective-permute-done.22
  153.3 1.0 fusion.82
  154.3 0.1 copy.8
  154.4 1.0 stack.3
  155.5 227.0 %all_to_all.5 = bf16[32,32,4096]{2,1,0:T(8,128)(2,1)S(1)} all-to-all(bf16[32,32,4096]{2,1,0:T(8,128)(2,1)S(1)} %stack.3), channel_id=1, replica_groups=mesh['dom'=16,'band'=32] {'band'}, dimensions={0} | all-to-all | bytes 16777216 | tf_op jit(solution)/shard_map/all_to_all | solution.py:19
  382.5 1.5 convolution_bitcast_fusion
  384.1 0.9 copy.6
  (29 shorter events, 0.4 us)
Async XLA Ops:
  0.0 382.5 %copy-start = (bf16[1024,32]{0,1:T(8,128)(2,1)S(1)}, bf16[1024,32]{0,1:T(8,128)(2,1)}, u32[]{:S(2)}) copy-start(bf16[1024,32]{0,1:T(8,128)(2,1)} %param.5) | copy-start | bytes 196612
  0.0 37.8 %copy-start.1 = (bf16[32,1,2,16,128]{4,3,2,1,0:T(8,128)(2,1)S(1)}, bf16[32,1,2,16,128]{4,3,2,1,0:T(8,128)(2,1)}, u32[]{:S(2)}) copy-start(bf16[32,1,2,16,128]{4,3,2,1,0:T(8,128)(2,1)} %param.3) | copy-start | bytes 786436
  0.0 21.3 %copy-start.2 = (f32[1,2,16,128]{3,2,1,0:T(8,128)S(1)}, f32[1,2,16,128]{3,2,1,0:T(8,128)}, u32[]{:S(2)}) copy-start(f32[1,2,16,128]{3,2,1,0:T(8,128)} %param.4) | copy-start | bytes 49156
  1.8 19.6 %collective-permute-start.3 = (f32[32,2,2,128]{3,2,1,0:T(2,128)}, f32[32,2,2,128]{3,2,1,0:T(2,128)}, u32[]{:S(2)}, u32[]{:S(2)}) collective-permute-start(f32[32,2,2,128]{3,2,1,0:T(2,128)} %get-tuple-element.37), channel_id=1, source_target_pairs={{0,32},{32,64},{64,96},{96,128},{128,160},{160,192},{192,224},{224... | collective-permute-start | bytes 196616 | tf_op jit(solution)/shard_map/ppermute | solution.py:35
  5.5 19.9 %collective-permute-start.2 = (f32[32,2,2,128]{3,2,1,0:T(2,128)}, f32[32,2,2,128]{3,2,1,0:T(2,128)}, u32[]{:S(2)}, u32[]{:S(2)}) collective-permute-start(f32[32,2,2,128]{3,2,1,0:T(2,128)} %get-tuple-element.37), channel_id=1, source_target_pairs={{0,416},{32,448},{64,480},{96,0},{128,32},{160,64},{192,96},{224,1... | collective-permute-start | bytes 196616 | tf_op jit(solution)/shard_map/ppermute | solution.py:35
  7.4 30.4 %collective-permute-start.1 = (f32[32,2,16,128]{3,2,1,0:T(8,128)S(1)}, f32[32,2,16,128]{3,2,1,0:T(8,128)}, u32[]{:S(2)}, u32[]{:S(2)}) collective-permute-start(f32[32,2,16,128]{3,2,1,0:T(8,128)S(1)} %bitcast_convert_fusion), channel_id=1, source_target_pairs={{0,384},{32,416},{64,448},{96,480},{128,0},{160,32},{192,64},{224,... | collective-permute-start | bytes 1572872 | tf_op jit(solution)/shard_map/ppermute | solution.py:35
  11.0 26.8 %collective-permute-start = (f32[32,2,16,128]{3,2,1,0:T(8,128)S(1)}, f32[32,2,16,128]{3,2,1,0:T(8,128)}, u32[]{:S(2)}, u32[]{:S(2)}) collective-permute-start(f32[32,2,16,128]{3,2,1,0:T(8,128)S(1)} %bitcast_convert_fusion), channel_id=1, source_target_pairs={{0,128},{32,160},{64,192},{96,224},{128,256},{160,288},{192,320},{... | collective-permute-start | bytes 1572872 | tf_op jit(solution)/shard_map/ppermute | solution.py:35
  14.2 23.0 %collective-permute-start.5 = (f32[32,2,2,128]{3,2,1,0:T(2,128)}, f32[32,2,2,128]{3,2,1,0:T(2,128)}, u32[]{:S(2)}, u32[]{:S(2)}) collective-permute-start(f32[32,2,2,128]{3,2,1,0:T(2,128)} %get-tuple-element.38), channel_id=1, source_target_pairs={{0,480},{32,0},{64,32},{96,64},{128,96},{160,128},{192,160},{224,1... | collective-permute-start | bytes 196616 | tf_op jit(solution)/shard_map/ppermute | solution.py:35
  21.4 16.4 %collective-permute-start.4 = (f32[32,2,2,128]{3,2,1,0:T(2,128)}, f32[32,2,2,128]{3,2,1,0:T(2,128)S(1)}, u32[]{:S(2)}, u32[]{:S(2)}) collective-permute-start(f32[32,2,2,128]{3,2,1,0:T(2,128)} %get-tuple-element.38), channel_id=1, source_target_pairs={{0,96},{32,128},{64,160},{96,192},{128,224},{160,256},{192,288},{2... | collective-permute-start | bytes 196616 | tf_op jit(solution)/shard_map/ppermute | solution.py:35
  40.7 17.8 %collective-permute-start.9 = (f32[32,2,2,128]{3,2,1,0:T(2,128)S(1)}, f32[32,2,2,128]{3,2,1,0:T(2,128)S(1)}, u32[]{:S(2)}, u32[]{:S(2)}) collective-permute-start(f32[32,2,2,128]{3,2,1,0:T(2,128)S(1)} %get-tuple-element.35), channel_id=1, source_target_pairs={{0,32},{32,64},{64,96},{96,128},{128,160},{160,192},{192,224},{224... | collective-permute-start | bytes 196616 | tf_op jit(solution)/shard_map/ppermute | solution.py:35
  45.1 18.1 %collective-permute-start.8 = (f32[32,2,2,128]{3,2,1,0:T(2,128)S(1)}, f32[32,2,2,128]{3,2,1,0:T(2,128)S(1)}, u32[]{:S(2)}, u32[]{:S(2)}) collective-permute-start(f32[32,2,2,128]{3,2,1,0:T(2,128)S(1)} %get-tuple-element.35), channel_id=1, source_target_pairs={{0,416},{32,448},{64,480},{96,0},{128,32},{160,64},{192,96},{224,1... | collective-permute-start | bytes 196616 | tf_op jit(solution)/shard_map/ppermute | solution.py:35
  47.1 30.6 %collective-permute-start.7 = (f32[32,2,16,128]{3,2,1,0:T(8,128)S(1)}, f32[32,2,16,128]{3,2,1,0:T(8,128)S(1)}, u32[]{:S(2)}, u32[]{:S(2)}) collective-permute-start(f32[32,2,16,128]{3,2,1,0:T(8,128)S(1)} %get-tuple-element.5), channel_id=1, source_target_pairs={{0,384},{32,416},{64,448},{96,480},{128,0},{160,32},{192,64},{224,... | collective-permute-start | bytes 1572872 | tf_op jit(solution)/shard_map/ppermute | solution.py:35
  50.0 27.8 %collective-permute-start.6 = (f32[32,2,16,128]{3,2,1,0:T(8,128)S(1)}, f32[32,2,16,128]{3,2,1,0:T(8,128)S(1)}, u32[]{:S(2)}, u32[]{:S(2)}) collective-permute-start(f32[32,2,16,128]{3,2,1,0:T(8,128)S(1)} %get-tuple-element.5), channel_id=1, source_target_pairs={{0,128},{32,160},{64,192},{96,224},{128,256},{160,288},{192,320},{... | collective-permute-start | bytes 1572872 | tf_op jit(solution)/shard_map/ppermute | solution.py:35
  54.7 22.0 %collective-permute-start.11 = (f32[32,2,2,128]{3,2,1,0:T(2,128)S(1)}, f32[32,2,2,128]{3,2,1,0:T(2,128)S(1)}, u32[]{:S(2)}, u32[]{:S(2)}) collective-permute-start(f32[32,2,2,128]{3,2,1,0:T(2,128)S(1)} %get-tuple-element.36), channel_id=1, source_target_pairs={{0,480},{32,0},{64,32},{96,64},{128,96},{160,128},{192,160},{224,1... | collective-permute-start | bytes 196616 | tf_op jit(solution)/shard_map/ppermute | solution.py:35
  58.6 19.1 %collective-permute-start.10 = (f32[32,2,2,128]{3,2,1,0:T(2,128)S(1)}, f32[32,2,2,128]{3,2,1,0:T(2,128)S(1)}, u32[]{:S(2)}, u32[]{:S(2)}) collective-permute-start(f32[32,2,2,128]{3,2,1,0:T(2,128)S(1)} %get-tuple-element.36), channel_id=1, source_target_pairs={{0,96},{32,128},{64,160},{96,192},{128,224},{160,256},{192,288},{2... | collective-permute-start | bytes 196616 | tf_op jit(solution)/shard_map/ppermute | solution.py:35
  78.9 19.0 %collective-permute-start.15 = (f32[32,2,2,128]{3,2,1,0:T(2,128)S(1)}, f32[32,2,2,128]{3,2,1,0:T(2,128)S(1)}, u32[]{:S(2)}, u32[]{:S(2)}) collective-permute-start(f32[32,2,2,128]{3,2,1,0:T(2,128)S(1)} %get-tuple-element.25), channel_id=1, source_target_pairs={{0,32},{32,64},{64,96},{96,128},{128,160},{160,192},{192,224},{224... | collective-permute-start | bytes 196616 | tf_op jit(solution)/shard_map/ppermute | solution.py:35
  82.4 18.1 %collective-permute-start.14 = (f32[32,2,2,128]{3,2,1,0:T(2,128)S(1)}, f32[32,2,2,128]{3,2,1,0:T(2,128)S(1)}, u32[]{:S(2)}, u32[]{:S(2)}) collective-permute-start(f32[32,2,2,128]{3,2,1,0:T(2,128)S(1)} %get-tuple-element.25), channel_id=1, source_target_pairs={{0,416},{32,448},{64,480},{96,0},{128,32},{160,64},{192,96},{224,1... | collective-permute-start | bytes 196616 | tf_op jit(solution)/shard_map/ppermute | solution.py:35
  84.6 30.6 %collective-permute-start.13 = (f32[32,2,16,128]{3,2,1,0:T(8,128)S(1)}, f32[32,2,16,128]{3,2,1,0:T(8,128)S(1)}, u32[]{:S(2)}, u32[]{:S(2)}) collective-permute-start(f32[32,2,16,128]{3,2,1,0:T(8,128)S(1)} %fusion.34), channel_id=1, source_target_pairs={{0,384},{32,416},{64,448},{96,480},{128,0},{160,32},{192,64},{224,... | collective-permute-start | bytes 1572872 | tf_op jit(solution)/shard_map/ppermute | solution.py:35
  89.2 26.0 %collective-permute-start.12 = (f32[32,2,16,128]{3,2,1,0:T(8,128)S(1)}, f32[32,2,16,128]{3,2,1,0:T(8,128)S(1)}, u32[]{:S(2)}, u32[]{:S(2)}) collective-permute-start(f32[32,2,16,128]{3,2,1,0:T(8,128)S(1)} %fusion.34), channel_id=1, source_target_pairs={{0,128},{32,160},{64,192},{96,224},{128,256},{160,288},{192,320},{... | collective-permute-start | bytes 1572872 | tf_op jit(solution)/shard_map/ppermute | solution.py:35
  92.3 22.0 %collective-permute-start.17 = (f32[32,2,2,128]{3,2,1,0:T(2,128)S(1)}, f32[32,2,2,128]{3,2,1,0:T(2,128)S(1)}, u32[]{:S(2)}, u32[]{:S(2)}) collective-permute-start(f32[32,2,2,128]{3,2,1,0:T(2,128)S(1)} %get-tuple-element.26), channel_id=1, source_target_pairs={{0,480},{32,0},{64,32},{96,64},{128,96},{160,128},{192,160},{224,1... | collective-permute-start | bytes 196616 | tf_op jit(solution)/shard_map/ppermute | solution.py:35
  97.8 17.4 %collective-permute-start.16 = (f32[32,2,2,128]{3,2,1,0:T(2,128)S(1)}, f32[32,2,2,128]{3,2,1,0:T(2,128)S(1)}, u32[]{:S(2)}, u32[]{:S(2)}) collective-permute-start(f32[32,2,2,128]{3,2,1,0:T(2,128)S(1)} %get-tuple-element.26), channel_id=1, source_target_pairs={{0,96},{32,128},{64,160},{96,192},{128,224},{160,256},{192,288},{2... | collective-permute-start | bytes 196616 | tf_op jit(solution)/shard_map/ppermute | solution.py:35
  116.3 17.8 %collective-permute-start.21 = (f32[32,2,2,128]{3,2,1,0:T(2,128)S(1)}, f32[32,2,2,128]{3,2,1,0:T(2,128)S(1)}, u32[]{:S(2)}, u32[]{:S(2)}) collective-permute-start(f32[32,2,2,128]{3,2,1,0:T(2,128)S(1)} %get-tuple-element.7), channel_id=1, source_target_pairs={{0,32},{32,64},{64,96},{96,128},{128,160},{160,192},{192,224},{224... | collective-permute-start | bytes 196616 | tf_op jit(solution)/shard_map/ppermute | solution.py:35
  119.9 18.1 %collective-permute-start.20 = (f32[32,2,2,128]{3,2,1,0:T(2,128)S(1)}, f32[32,2,2,128]{3,2,1,0:T(2,128)S(1)}, u32[]{:S(2)}, u32[]{:S(2)}) collective-permute-start(f32[32,2,2,128]{3,2,1,0:T(2,128)S(1)} %get-tuple-element.7), channel_id=1, source_target_pairs={{0,416},{32,448},{64,480},{96,0},{128,32},{160,64},{192,96},{224,1... | collective-permute-start | bytes 196616 | tf_op jit(solution)/shard_map/ppermute | solution.py:35
  121.9 31.4 %collective-permute-start.19 = (f32[32,2,16,128]{3,2,1,0:T(8,128)S(1)}, f32[32,2,16,128]{3,2,1,0:T(8,128)S(1)}, u32[]{:S(2)}, u32[]{:S(2)}) collective-permute-start(f32[32,2,16,128]{3,2,1,0:T(8,128)S(1)} %fusion.22), channel_id=1, source_target_pairs={{0,384},{32,416},{64,448},{96,480},{128,0},{160,32},{192,64},{224,... | collective-permute-start | bytes 1572872 | tf_op jit(solution)/shard_map/ppermute | solution.py:35
  125.6 27.7 %collective-permute-start.18 = (f32[32,2,16,128]{3,2,1,0:T(8,128)S(1)}, f32[32,2,16,128]{3,2,1,0:T(8,128)S(1)}, u32[]{:S(2)}, u32[]{:S(2)}) collective-permute-start(f32[32,2,16,128]{3,2,1,0:T(8,128)S(1)} %fusion.22), channel_id=1, source_target_pairs={{0,128},{32,160},{64,192},{96,224},{128,256},{160,288},{192,320},{... | collective-permute-start | bytes 1572872 | tf_op jit(solution)/shard_map/ppermute | solution.py:35
  129.5 22.0 %collective-permute-start.23 = (f32[32,2,2,128]{3,2,1,0:T(2,128)S(1)}, f32[32,2,2,128]{3,2,1,0:T(2,128)S(1)}, u32[]{:S(2)}, u32[]{:S(2)}) collective-permute-start(f32[32,2,2,128]{3,2,1,0:T(2,128)S(1)} %get-tuple-element.8), channel_id=1, source_target_pairs={{0,480},{32,0},{64,32},{96,64},{128,96},{160,128},{192,160},{224,1... | collective-permute-start | bytes 196616 | tf_op jit(solution)/shard_map/ppermute | solution.py:35
  134.2 19.0 %collective-permute-start.22 = (f32[32,2,2,128]{3,2,1,0:T(2,128)S(1)}, f32[32,2,2,128]{3,2,1,0:T(2,128)S(1)}, u32[]{:S(2)}, u32[]{:S(2)}) collective-permute-start(f32[32,2,2,128]{3,2,1,0:T(2,128)S(1)} %get-tuple-element.8), channel_id=1, source_target_pairs={{0,96},{32,128},{64,160},{96,192},{128,224},{160,256},{192,288},{2... | collective-permute-start | bytes 196616 | tf_op jit(solution)/shard_map/ppermute | solution.py:35
